TPU v7x, 32 devices: a whole 2x2x4 slice. The times are simulated.
32 devices in a mesh: seq: 4 (over z), dp: 8 (over y, x, core).
Axes of the slice: x: 2, y: 2, z: 4, core: 2. Of those that a mesh axis runs over, the one named last changes fastest.
Arguments:
- hidden_in: bfloat16 [16, 2048, 1024], P('dp', 'seq'), may hold values from -6 to 6
- mixer_weights: float32 [1, 5, 1024, 1024], P(None, None, 'dp'), may hold values from -0.1875 to 0.1875
- channel_in_weights: float32 [1, 2, 1024, 2816], P(None, None, 'dp'), may hold values from -0.1875 to 0.1875
- channel_out_weights: float32 [1, 2816, 1024], P(None, 'dp'), may hold values from -0.109375 to 0.109375
- decay_rates: float32 [1, 8], replicated, may hold values from 0 to 0.034, as said below
- doc_lengths: int32 [16, 4], P('dp'), may hold values from 1 to 1024, 2048 in all within a row
- out_cotangent: bfloat16 [16, 2048, 1024], P('dp', 'seq'), may hold values from -6 to 6
Outputs:
- block_output: bfloat16 [16, 2048, 1024], P('dp', 'seq')
- input_gradient: float32 [16, 2048, 1024], P('dp', 'seq')
- mixer_gradient: float32 [1, 5, 1024, 1024], P(None, None, 'dp')
- channel_in_gradient: float32 [1, 2, 1024, 2816], P(None, None, 'dp')
- channel_out_gradient: float32 [1, 2816, 1024], P(None, 'dp')
Inputs may be any that keep to these rules, and one draw needn't show every extreme that they name: `decay_rates`: positive decay rates. `doc_lengths`: each row's 4 lengths add up to 2048.
All inputs are finite; a program needn't handle non-finite values.
Results may differ from a plain program's by a relative error of at most 0.02.
Values may be sent and summed in bfloat16 or wider, within the bound.
No kernel may reach another device: no remote copies, remote signals or barrier semaphores. Data moves between devices by JAX's collectives and lax.ppermute only.
A program may use at most 256 MiB of HBM per device.

v0:
```python
import jax
import jax.numpy as jnp
from jax import lax
from jax.sharding import PartitionSpec as P

EPS = 1e-06
FULL_PRECISION = lax.Precision.HIGHEST


def passed_along(value, axis, steps):
    count = lax.axis_size(axis)
    leading, last = (max(0, -steps), min(count, count - steps))
    return lax.ppermute(value, axis, [(source, source + steps) for source in range(leading, last)])


def product(left, right):
    return jnp.dot(left, right, preferred_element_type=jnp.float32)


def rms_norm(value_rows):
    factor = lax.rsqrt(jnp.mean(value_rows * value_rows, axis=-1, keepdims=True) + EPS)
    return (value_rows * factor, factor)


def norm_back(value_rows, factor, upstream):
    features = value_rows.shape[-1]
    inner_sum = jnp.sum(upstream * value_rows, axis=-1, keepdims=True)
    return factor * upstream - factor * factor * factor / features * value_rows * inner_sum


def swish_slope(value_rows):
    sigmoid_part = jax.nn.sigmoid(value_rows)
    return sigmoid_part * (1.0 + value_rows * (1.0 - sigmoid_part))


def doc_index(doc_ends, places):
    compare = places[None, :, None] >= doc_ends[:, None, :]
    return jnp.sum(compare.astype(jnp.int32), axis=-1, dtype=jnp.int32)


def decay_tables(rates, doc_ends, start, count):
    float_kind = rates.dtype
    offsets = jnp.arange(count, dtype=jnp.int32)
    start = jnp.asarray(start, dtype=jnp.int32)
    doc_here = doc_index(doc_ends, start + offsets)
    before_place = jnp.full((1,), -1, dtype=jnp.int32) + start
    doc_before = doc_index(doc_ends, before_place)[:, 0]
    doc_last = doc_here[:, count - 1]
    distance = jnp.maximum(offsets[:, None] - offsets[None, :], 0).astype(float_kind)
    causal = offsets[:, None] >= offsets[None, :]
    linked = causal[None] & (doc_here[:, :, None] == doc_here[:, None, :])
    intra_vals = jnp.exp(-rates[None, :, None, None] * distance[None, None])
    intra = jnp.where(linked[:, None], intra_vals, jnp.zeros_like(intra_vals))
    ahead = (offsets + 1).astype(float_kind)
    behind = (count - 1 - offsets).astype(float_kind)
    entry_vals = jnp.exp(-rates[None, None, :] * ahead[None, :, None])
    entry = jnp.where(
        (doc_here == doc_before[:, None])[:, :, None], entry_vals, jnp.zeros_like(entry_vals)
    )
    leaving_vals = jnp.exp(-rates[None, None, :] * behind[None, :, None])
    leaving = jnp.where(
        (doc_here == doc_last[:, None])[:, :, None], leaving_vals, jnp.zeros_like(leaving_vals)
    )
    length_value = jnp.asarray(count, dtype=float_kind)
    passing_vals = jnp.exp(-rates * length_value)[None, :] + jnp.zeros(
        (doc_last.shape[0], 1), float_kind
    )
    passing = jnp.where(
        (doc_last == doc_before)[:, None], passing_vals, jnp.zeros_like(passing_vals)
    )
    return (intra, entry, leaving, passing)


def block_out(per_head_queries, per_head_keys, per_head_values, tables, state_in):
    scores = (
        jnp.einsum("rthd,rshd->rhts", per_head_queries, per_head_keys, precision=FULL_PRECISION)
        * tables[0]
    )
    local_part = jnp.einsum("rhts,rshe->rthe", scores, per_head_values, precision=FULL_PRECISION)
    carried = (
        jnp.einsum("rthd,rhde->rthe", per_head_queries, state_in, precision=FULL_PRECISION)
        * tables[1][..., None]
    )
    return local_part + carried


def block_state(per_head_keys, per_head_values, tables):
    return jnp.einsum(
        "rshd,rshe->rhde",
        per_head_keys * tables[2][..., None],
        per_head_values,
        precision=FULL_PRECISION,
    )


def block_back(
    per_head_queries, per_head_keys, per_head_values, upstream, tables, state_in, state_grad
):
    intra, entry, leaving, passing = tables
    scores = (
        jnp.einsum("rthd,rshd->rhts", per_head_queries, per_head_keys, precision=FULL_PRECISION)
        * intra
    )
    score_grad = (
        jnp.einsum("rthe,rshe->rhts", upstream, per_head_values, precision=FULL_PRECISION) * intra
    )
    query_grad = jnp.einsum("rhts,rshd->rthd", score_grad, per_head_keys, precision=FULL_PRECISION)
    query_grad = (
        query_grad
        + jnp.einsum("rthe,rhde->rthd", upstream, state_in, precision=FULL_PRECISION)
        * entry[..., None]
    )
    key_grad = jnp.einsum("rhts,rthd->rshd", score_grad, per_head_queries, precision=FULL_PRECISION)
    key_grad = (
        key_grad
        + jnp.einsum("rshe,rhde->rshd", per_head_values, state_grad, precision=FULL_PRECISION)
        * leaving[..., None]
    )
    value_grad = jnp.einsum("rhts,rthe->rshe", scores, upstream, precision=FULL_PRECISION)
    value_grad = (
        value_grad
        + jnp.einsum("rshd,rhde->rshe", per_head_keys, state_grad, precision=FULL_PRECISION)
        * leaving[..., None]
    )
    return (query_grad, key_grad, value_grad)


def carry_forward(passing, local_state):

    def step_forward(turn_index, incoming):
        outgoing = passing[..., None, None] * incoming + local_state
        return passed_along(outgoing.astype(jnp.bfloat16), "seq", 1).astype(outgoing.dtype)

    return lax.fori_loop(0, lax.axis_size("seq") - 1, step_forward, jnp.zeros_like(local_state))


def carry_backward(passing, local_grad):

    def retreat(turn_index, incoming):
        outgoing = passing[..., None, None] * incoming + local_grad
        return passed_along(outgoing.astype(jnp.bfloat16), "seq", -1).astype(outgoing.dtype)

    return lax.fori_loop(0, lax.axis_size("seq") - 1, retreat, jnp.zeros_like(local_grad))


def reduce_grads(terms):
    pieces = (
        lax.psum_scatter(
            terms[0].astype(jnp.bfloat16), "dp", scatter_dimension=1, tiled=True
        ).astype(jnp.float32),
        lax.psum_scatter(
            terms[1].astype(jnp.bfloat16), "dp", scatter_dimension=0, tiled=True
        ).astype(jnp.float32),
        lax.psum_scatter(
            terms[2].astype(jnp.bfloat16), "dp", scatter_dimension=1, tiled=True
        ).astype(jnp.float32),
        lax.psum_scatter(
            terms[3].astype(jnp.bfloat16), "dp", scatter_dimension=0, tiled=True
        ).astype(jnp.float32),
    )
    return (
        lax.psum(pieces[0].astype(jnp.bfloat16), "seq").astype(jnp.float32),
        lax.psum(pieces[1].astype(jnp.bfloat16), "seq").astype(jnp.float32),
        lax.psum(pieces[2].astype(jnp.bfloat16), "seq").astype(jnp.float32),
        lax.psum(pieces[3].astype(jnp.bfloat16), "seq").astype(jnp.float32),
    )


def local(
    hidden_in,
    mixer_weights,
    channel_in_weights,
    channel_out_weights,
    decay_rates,
    doc_lengths,
    out_cotangent,
):
    rows, tokens, features = hidden_in.shape
    layers = mixer_weights.shape[0]
    heads = decay_rates.shape[1]
    head_dim = features // heads
    count = rows * tokens
    head_shape = (rows, tokens, heads, head_dim)
    start = lax.axis_index("seq") * jnp.asarray(tokens, dtype=jnp.int32)
    doc_ends = jnp.cumsum(doc_lengths, axis=1, dtype=jnp.int32)
    resid = hidden_in.astype(jnp.float32).reshape(count, features)
    layer_index = 0
    gathered = (
        mixer_weights[layer_index].astype(jnp.bfloat16),
        channel_in_weights[layer_index].astype(jnp.bfloat16),
        channel_out_weights[layer_index].astype(jnp.bfloat16),
    )
    mixer_full = lax.all_gather(gathered[0], "dp", axis=1, tiled=True)
    channel_full = lax.all_gather(gathered[1], "dp", axis=1, tiled=True)
    down_full = lax.all_gather(gathered[2], "dp", axis=0, tiled=True)
    normed, factor_in = rms_norm(resid)
    normed_low = normed.astype(jnp.bfloat16)
    projected = jnp.einsum(
        "nd,kde->kne", normed_low, mixer_full[:4], preferred_element_type=jnp.float32
    )
    query_pre = projected[0]
    key_pre = projected[1]
    value_pre = projected[2]
    gate_pre = projected[3]
    per_head_queries = (query_pre * jax.nn.sigmoid(query_pre)).reshape(head_shape)
    per_head_keys = (key_pre * jax.nn.sigmoid(key_pre)).reshape(head_shape)
    per_head_values = value_pre.reshape(head_shape)
    tables = decay_tables(decay_rates[layer_index], doc_ends, start, tokens)
    local_state = block_state(per_head_keys, per_head_values, tables)
    state_in = carry_forward(tables[3], local_state)
    mixed = block_out(per_head_queries, per_head_keys, per_head_values, tables, state_in).reshape(
        count, features
    )
    mixed_norm, factor_mix = rms_norm(mixed)
    gated = (mixed_norm * gate_pre).astype(jnp.bfloat16)
    after_mixer = resid + product(gated, mixer_full[4])
    normed_two, factor_two = rms_norm(after_mixer)
    normed_two_low = normed_two.astype(jnp.bfloat16)
    pair = jnp.einsum(
        "nd,kdf->knf", normed_two_low, channel_full, preferred_element_type=jnp.float32
    )
    glu = (pair[0] * pair[1]).astype(jnp.bfloat16)
    saved = [
        (
            mixer_full,
            channel_full,
            down_full,
            resid,
            factor_in,
            normed_low,
            query_pre,
            key_pre,
            gate_pre,
            per_head_queries,
            per_head_keys,
            per_head_values,
            tables,
            state_in,
            mixed,
            mixed_norm,
            factor_mix,
            gated,
            after_mixer,
            factor_two,
            normed_two_low,
            pair,
            glu,
        )
    ]
    resid = after_mixer + product(glu, down_full)
    block_output = resid.astype(jnp.bfloat16).reshape(rows, tokens, features)
    upstream = out_cotangent.astype(jnp.float32).reshape(count, features)
    mixer_list = []
    channel_list = []
    down_list = []
    for layer_index in reversed(range(layers)):
        (
            mixer_full,
            channel_full,
            down_full,
            resid_in,
            factor_in,
            normed_low,
            query_pre,
            key_pre,
            gate_pre,
            per_head_queries,
            per_head_keys,
            per_head_values,
            tables,
            state_in,
            mixed,
            mixed_norm,
            factor_mix,
            gated,
            after_mixer,
            factor_two,
            normed_two_low,
            pair,
            glu,
        ) = saved[layer_index]
        branch_low = upstream.astype(jnp.bfloat16)
        down_term = jnp.einsum("nf,nd->fd", glu, branch_low, preferred_element_type=jnp.float32)
        glu_grad = (
            jnp.einsum("nd,fd->nf", branch_low, down_full, preferred_element_type=jnp.float32)
            .astype(jnp.bfloat16)
            .astype(jnp.float32)
        )
        pair_grad = jnp.stack([glu_grad * pair[1], glu_grad * pair[0]]).astype(jnp.bfloat16)
        channel_term = jnp.einsum(
            "nd,knf->kdf", normed_two_low, pair_grad, preferred_element_type=jnp.float32
        )
        two_grad = jnp.einsum(
            "knf,kdf->nd", pair_grad, channel_full, preferred_element_type=jnp.float32
        )
        upstream_mid = upstream + norm_back(after_mixer, factor_two, two_grad)
        mixer_low = upstream_mid.astype(jnp.bfloat16)
        out_term = jnp.einsum("nd,ne->de", gated, mixer_low, preferred_element_type=jnp.float32)
        gated_grad = (
            jnp.einsum("ne,de->nd", mixer_low, mixer_full[4], preferred_element_type=jnp.float32)
            .astype(jnp.bfloat16)
            .astype(jnp.float32)
        )
        gate_grad = gated_grad * mixed_norm
        mixed_grad = norm_back(mixed, factor_mix, gated_grad * gate_pre).reshape(head_shape)
        local_grad = jnp.einsum(
            "rthd,rthe->rhde",
            per_head_queries * tables[1][..., None],
            mixed_grad,
            precision=FULL_PRECISION,
        )
        state_grad = carry_backward(tables[3], local_grad)
        query_grad, key_grad, value_grad = block_back(
            per_head_queries,
            per_head_keys,
            per_head_values,
            mixed_grad,
            tables,
            state_in,
            state_grad,
        )
        proj_grad = jnp.stack(
            [
                query_grad.reshape(count, features) * swish_slope(query_pre),
                key_grad.reshape(count, features) * swish_slope(key_pre),
                value_grad.reshape(count, features),
                gate_grad,
            ]
        ).astype(jnp.bfloat16)
        four_term = jnp.einsum(
            "nd,kne->kde", normed_low, proj_grad, preferred_element_type=jnp.float32
        )
        one_grad = jnp.einsum(
            "kne,kde->nd", proj_grad, mixer_full[:4], preferred_element_type=jnp.float32
        )
        upstream = upstream_mid + norm_back(resid_in, factor_in, one_grad)
        summed = reduce_grads((four_term, out_term, channel_term, down_term))
        mixer_list.append(jnp.concatenate([summed[0], summed[1][None]], axis=0))
        channel_list.append(summed[2])
        down_list.append(summed[3])
    mixer_gradient = jnp.stack(mixer_list[::-1])
    channel_in_gradient = jnp.stack(channel_list[::-1])
    channel_out_gradient = jnp.stack(down_list[::-1])
    input_gradient = upstream.reshape(rows, tokens, features)
    return (block_output, input_gradient, mixer_gradient, channel_in_gradient, channel_out_gradient)


def solution(mesh):
    in_specs = (
        P("dp", "seq", None),
        P(None, None, "dp", None),
        P(None, None, "dp", None),
        P(None, "dp", None),
        P(),
        P("dp", None),
        P("dp", "seq", None),
    )
    out_specs = (
        P("dp", "seq", None),
        P("dp", "seq", None),
        P(None, None, "dp", None),
        P(None, None, "dp", None),
        P(None, "dp", None),
    )
    return jax.shard_map(local, mesh=mesh, in_specs=in_specs, out_specs=out_specs, check_vma=False)
```

profile of v0, /device:TPU:0, one launch (start us, length us, event | category | flops | bytes accessed | tf_op | source)
XLA Modules:
  0.0 966.9 jit_solution(12912789637610193381)
XLA Ops:
  26.6 51.9 %all-gather.7.cloned.1.call-done = bf16[1,5,1024,1024]{2,3,1,0:T(8,128)(2,1)} async-done(((bf16[1,5,128,1024]{2,3,1,0:T(8,128)(2,1)}), bf16[1,5,1024,1024]{2,3,1,0:T(8,128)(2,1)}) %all-gather.7.cloned.1.call-update) | async-done | bytes 10485776 | tf_op jit(solution)/shard_map/all_gather | solution.py:193
  78.5 16.3 %convolution_bitcast_fusion = f32[4,1024,1024]{1,2,0:T(8,128)} fusion(bf16[1,5,1024,1024]{2,3,1,0:T(8,128)(2,1)} %all-gather.7.cloned.1.call-done, bf16[1024,1024]{1,0:T(8,128)(2,1)} %fusion.65), kind=kOutput, calls=%fused_computation.30 | convolution fusion | flops 8589934592 | bytes 27262976 | tf_op jit(solution)/shard_map/nd,kde->kne/dot_general | solution.py:198
  140.8 48.7 %while.22 = (s32[]{:T(128)}, f32[2,8,128,128]{3,2,1,0:T(8,128)S(1)}, f32[2,8,128,128]{3,2,1,0:T(8,128)S(1)}, f32[8]{0:T(128)S(1)}, pred[2]{0:T(512)(128)(4,1)S(1)}, /*index=5*/s32[]{:T(128)}, s32[]{:T(128)}) while((s32[]{:T(128)}, f32[2,8,128,128]{3,2,1,0:T(8,128)S(1)}, f32[2,8,128,128]{3,2,1,0:T(8,128)S(1)}, f32[8]{0:T(128)S(1)}, ...), condition=%wide.region_5.6_spmd.clone, body=%wide.region_4.5_spmd.clone.sunk | while | flops 1310739 | bytes 6291745 | solution.py:134
  198.8 17.2 %fusion.118 = f32[2,8,512,512]{3,2,1,0:T(8,128)} fusion(f32[2,512,8,128]{1,0,3,2:T(2,128)S(1)} %copy-done.14, f32[2,512,8,128]{1,0,3,2:T(2,128)S(1)} %copy-done.13), kind=kOutput, calls=%fused_computation.164 | convolution fusion | flops 6450839552 | bytes 25165824 | tf_op jit(solution)/shard_map/rthd,rshd->rhts/dot_general | solution.py:76
  216.0 23.7 %multiply_reduce_fusion.2 = (f32[2,512]{1,0:T(2,128)S(1)}, f32[2,512,8,128]{1,3,2,0:T(8,128)}) fusion(f32[2,512,8]{1,2,0:T(8,128)S(1)} %get-tuple-element.166, f32[2,8,128,512]{3,2,1,0:T(8,128)} %fusion.119, f32[2,512,8,128]{3,1,2,0:T(8,128)} %copy.119, f32[2,8,512,512]{3,2,1,0:T(8,128)} %fusion.118, f32[8,512,512]{2,1,0:T(8,128)} %multiply_exponential_fusion, ...), kind=kOutput, calls=%fused_computation.99 | convolution fusion | flops 6455032832 | bytes 38309888 | tf_op jit(solution)/shard_map/rhts,rshe->rthe/dot_general | solution.py:79
  267.0 20.9 %fusion.19 = f32[2,1024,2816]{2,1,0:T(8,128)} fusion(bf16[1,2,1024,2816]{3,2,1,0:T(8,128)(2,1)} %all-gather.9.cloned.1.call-done, f32[1024,1024]{1,0:T(8,128)} %get-tuple-element.159, f32[1024]{0:T(1024)S(1)} %get-tuple-element.149), kind=kOutput, calls=%fused_computation.29 | convolution fusion | flops 11813257216 | bytes 38801408 | tf_op jit(solution)/shard_map/nd,kdf->knf/dot_general | solution.py:219
  287.9 14.9 %fusion.41 = (bf16[1,1024,2816]{2,1,0:T(8,128)(2,1)}, bf16[1,1024,2816]{2,1,0:T(8,128)(2,1)}) fusion(f32[2,1024,2816]{2,1,0:T(8,128)} %fusion.19, bf16[1024,1024]{1,0:T(8,128)(2,1)S(1)} %bitcast.231, bf16[1,2816,1024]{2,1,0:T(8,128)(2,1)} %all-gather.11.cloned.1.call-done), kind=kOutput, calls=%fused_computation.52 | convolution fusion | flops 5922881536 | bytes 42467328 | tf_op jit(solution)/shard_map/nd,fd->nf/dot_general | solution.py:285
  302.9 20.3 %fusion.62 = (f32[1024]{0:T(1024)S(1)}, f32[1024,1024,1]{1,0,2:T(8,128)}) fusion(f32[1024,1024]{1,0:T(8,128)} %get-tuple-element.159, bf16[1,2,1024,2816]{3,2,1,0:T(8,128)(2,1)} %all-gather.9.cloned.1.call-done, bf16[1,1024,2816]{2,1,0:T(8,128)(2,1)} %get-tuple-element.140, bf16[1,1024,2816]{2,1,0:T(8,128)(2,1)} %get-tuple-element.139), kind=kOutput, calls=%fused_computation.79 | convolution fusion | flops 11819023360 | bytes 31461376 | tf_op jit(solution)/shard_map/knf,kdf->nd/dot_general | solution.py:293
  348.0 19.9 %fusion.8 = f32[2,8,128,512]{3,2,1,0:T(8,128)} fusion(f32[2,8,512,512]{3,2,1,0:T(8,128)} %fusion.118, f32[8,512,512]{2,1,0:T(8,128)} %multiply_exponential_fusion, pred[2,512,512]{2,1,0:T(8,128)(4,1)S(1)} %compare_and_fusion, f32[2,512,8,128]{1,0,3,2:T(2,128)} %reshape.344), kind=kOutput, calls=%fused_computation.12 | convolution fusion | flops 6450839552 | bytes 34078720 | tf_op jit(solution)/shard_map/rhts,rthe->rshe/dot_general | solution.py:119
  376.8 16.0 %fusion.74 = f32[2,8,512,512]{3,2,1,0:T(8,128)} fusion(f32[2,512,8,128]{3,1,2,0:T(8,128)S(1)} %copy-done.5, f32[2,512,8,128]{1,0,3,2:T(2,128)S(1)} %copy-done.6), kind=kOutput, calls=%fused_computation.107 | convolution fusion | flops 6442450944 | bytes 25165824 | tf_op jit(solution)/shard_map/rthe,rshe->rhts/dot_general | solution.py:105
  398.8 43.1 %while.23 = (s32[]{:T(128)}, f32[2,8,128,128]{3,2,1,0:T(8,128)S(1)}, f32[2,8,128,128]{3,2,1,0:T(8,128)S(1)}, f32[8]{0:T(128)S(1)}, pred[2]{0:T(512)(128)(4,1)S(1)}, /*index=5*/s32[]{:T(128)}, s32[]{:T(128)}) while((s32[]{:T(128)}, f32[2,8,128,128]{3,2,1,0:T(8,128)S(1)}, f32[2,8,128,128]{3,2,1,0:T(8,128)S(1)}, f32[8]{0:T(128)S(1)}, ...), condition=%wide.region_11.12_spmd.clone, body=%wide.region_10.11_spmd.clone.sunk | while | flops 1310739 | bytes 6291745 | solution.py:143
  401.1 13.0 %collective-permute-done.1 = bf16[2,8,128,128]{3,2,1,0:T(8,128)(2,1)S(1)} collective-permute-done((bf16[2,8,128,128]{3,2,1,0:T(8,128)(2,1)}, bf16[2,8,128,128]{3,2,1,0:T(8,128)(2,1)S(1)}, u32[]{:S(2)}, u32[]{:S(2)}) %collective-permute-start.1) | collective-permute-done | bytes 524320 | tf_op jit(solution)/shard_map/while/body/eval_jaxpr/ppermute | solution.py:13
  459.8 28.1 %fusion.11 = f32[2,8,128,512]{3,2,1,0:T(8,128)} fusion(f32[2,8,512,512]{3,2,1,0:T(8,128)} %fusion.74, f32[8,512,512]{2,1,0:T(8,128)} %multiply_exponential_fusion, pred[2,512,512]{2,1,0:T(8,128)(4,1)S(1)} %compare_and_fusion, f32[2,512,8,128]{1,0,3,2:T(2,128)} %squeeze.13), kind=kOutput, calls=%fused_computation.15 | convolution fusion | flops 6455033856 | bytes 34078720 | tf_op jit(solution)/shard_map/rhts,rshd->rthd/dot_general | solution.py:107
  508.2 21.7 %fusion.57 = f32[2,512,8,128]{1,3,2,0:T(8,128)} fusion(f32[2,8,128,512]{3,2,1,0:T(8,128)} %fusion.123, f32[2,8,512,512]{3,2,1,0:T(8,128)} %fusion.74, f32[8,512,512]{2,1,0:T(8,128)} %multiply_exponential_fusion, pred[2,512,512]{2,1,0:T(8,128)(4,1)S(1)} %compare_and_fusion, f32[2,512,8]{1,2,0:T(8,128)S(1)} %copy-done.28, f32[2,512,8,128]{1,0,3,2:T(2,128)} %squeeze.12), kind=kOutput, calls=%fused_computation.70 | convolution fusion | flops 6457131008 | bytes 38305792 | tf_op jit(solution)/shard_map/rhts,rthd->rshd/dot_general | solution.py:113
  565.5 15.0 %copy.151 = bf16[4,1024,1024]{2,0,1:T(4,128)(2,1)} copy(bf16[4,1024,1024]{1,2,0:T(8,128)(2,1)} %convert_bitcast_fusion.1) | data formatting | bytes 16777216
  580.5 12.3 %copy.160 = bf16[128,8,4,1024]{3,1,2,0:T(8,128)(2,1)} copy(bf16[128,8,4,1024]{3,2,1,0:T(4,128)(2,1)} %bitcast.226) | data formatting | bytes 16777216
  592.8 19.1 %convert_bitcast_fusion = bf16[2,1024,2816]{1,2,0:T(8,128)(2,1)} fusion(bf16[1,1024,2816]{2,1,0:T(8,128)(2,1)} %get-tuple-element.140, bf16[1,1024,2816]{2,1,0:T(8,128)(2,1)} %get-tuple-element.139, f32[1024,1024]{1,0:T(8,128)} %get-tuple-element.159, f32[1024]{0:T(1024)S(1)} %get-tuple-element.149), kind=kOutput, calls=%fused_computation.28 | convolution fusion | flops 11824791552 | bytes 27267072 | tf_op jit(solution)/shard_map/nd,knf->kdf/dot_general | solution.py:290
  611.9 29.1 %copy.155 = bf16[2,1024,2816]{2,0,1:T(2,128)(2,1)} copy(bf16[2,1024,2816]{1,2,0:T(8,128)(2,1)} %convert_bitcast_fusion) | data formatting | bytes 23068672
  654.0 15.9 %fusion.45 = bf16[2816,1024]{1,0:T(8,128)(2,1)} fusion(bf16[1024,1024]{1,0:T(8,128)(2,1)S(1)} %bitcast.232, f32[2,1024,2816]{2,1,0:T(8,128)} %fusion.19), kind=kOutput, calls=%fused_computation.56 | convolution fusion | flops 5914230784 | bytes 30932992 | tf_op jit(solution)/shard_map/nf,nd->fd/dot_general | solution.py:283
  676.2 76.9 %reduce-scatter.17.cloned.1.call-done = bf16[128,5632]{1,0:T(8,128)(2,1)} async-done(((bf16[1024,5632]{1,0:T(8,128)(2,1)}), bf16[128,5632]{1,0:T(8,128)(2,1)}) %reduce-scatter.17.cloned.1.call-update) | async-done | bytes 1441808
  759.6 56.0 %reduce-scatter.11.cloned.1.call-done = bf16[352,1024]{1,0:T(8,128)(2,1)} async-done(((bf16[2816,1024]{1,0:T(8,128)(2,1)}), bf16[352,1024]{1,0:T(8,128)(2,1)}) %reduce-scatter.11.cloned.1.call-update) | async-done | bytes 720912 | tf_op jit(solution)/shard_map/reduce_scatter | solution.py:157
  815.7 15.1 %fusion.54 = (f32[1024]{0:T(1024)S(1)}, f32[1024,1024,1]{1,0,2:T(8,128)S(1)}) fusion(bf16[2,512,1024]{2,1,0:T(8,128)(2,1)S(1)} %copy-done.12, bf16[1,5,1024,1024]{2,3,1,0:T(8,128)(2,1)} %all-gather.7.cloned.1.call-done, bf16[1,1024,1024]{1,2,0:T(8,128)(2,1)} %get-tuple-element.147, bf16[1,1024,1024]{1,2,0:T(8,128)(2,1)} %stack_reshape.4, ...), kind=kOutput, calls=%fused_computation.65 | convolution fusion | flops 8605662208 | bytes 23072768 | tf_op jit(solution)/shard_map/kne,kde->nd/dot_general | solution.py:333
  834.4 13.7 %add_convert_fusion = bf16[1024,1024]{1,0:T(8,128)(2,1)} fusion(f32[1024,1024]{1,0:T(8,128)S(1)} %copy-done.17, bf16[1,2816,1024]{2,1,0:T(8,128)(2,1)} %all-gather.11.cloned.1.call-done, f32[2,1024,2816]{2,1,0:T(8,128)} %fusion.19), kind=kOutput, calls=%fused_computation.95 | convolution fusion | flops 5913444352 | bytes 35127296 | tf_op jit(solution)/shard_map/dot_general | solution.py:17
  848.1 103.7 %all-reduce.3.cloned.1.call-done = (bf16[1,2,128,2816]{2,3,1,0:T(8,128)(2,1)}, bf16[1,128,1024]{1,2,0:T(8,128)(2,1)}, bf16[4,128,1024]{1,2,0:T(8,128)(2,1)}, bf16[1,352,1024]{2,1,0:T(8,128)(2,1)}) async-done(((bf16[1,2,128,2816]{2,3,1,0:T(8,128)(2,1)}, bf16[1,128,1024]{1,2,0:T(8,128)(2,1)}, bf16[4,128,1024]{1,2,0:T(8,128)(2,1)}, bf16[1,352,1024]{2,1,0:T(8,128)(2,1)}), (bf16[1,2,128,2816]{2,3,1,0:T(8,128)(2,1)}, ...) | async-done | bytes 3473424 | tf_op jit(solution)/shard_map/psum | solution.py:164
  (193 shorter events, 330.6 us)
Async XLA Ops:
  7.2 71.3 %all-gather.7.cloned.1.call-start = ((), (), s32[]{:S(2)}) async-start(), calls=%async_computation.5 | async-start | bytes 11796480 | tf_op jit(solution)/shard_map/all_gather | solution.py:193
  10.0 256.9 %all-gather.9.cloned.1.call-start = ((), (), s32[]{:S(2)}) async-start(), calls=%async_computation.6 | async-start | bytes 12976128 | tf_op jit(solution)/shard_map/all_gather | solution.py:194
  13.3 274.6 %all-gather.11.cloned.1.call-start = ((), (), s32[]{:S(2)}) async-start(), calls=%async_computation.7 | async-start | bytes 6488064 | tf_op jit(solution)/shard_map/all_gather | solution.py:195
  15.7 654.9 %reduce-scatter.15.cloned.1.call-start = ((), (), s32[]{:S(2)}) async-start(), calls=%async_computation.9 | async-start | bytes 2359296
  26.6 105.7 %copy-start.27 = (f32[2,512,8]{1,2,0:T(8,128)}, f32[2,512,8]{1,2,0:T(8,128)S(1)}, u32[]{:S(2)}) copy-start(f32[2,512,8]{1,2,0:T(8,128)S(1)} %get-tuple-element.167) | copy-start | bytes 98308
  141.9 15.3 %collective-permute-start = (bf16[2,8,128,128]{3,2,1,0:T(8,128)(2,1)}, bf16[2,8,128,128]{3,2,1,0:T(8,128)(2,1)S(1)}, u32[]{:S(2)}, u32[]{:S(2)}) collective-permute-start(bf16[2,8,128,128]{3,2,1,0:T(8,128)(2,1)} %fusion.136), channel_id=1, source_target_pairs={{0,8},{8,16},{16,24},{1,9},{9,17},{17,25},{2,10},{10,18},{18,26},{... | collective-permute-start | bytes 1572872 | tf_op jit(solution)/shard_map/while/body/eval_jaxpr/ppermute | solution.py:13
  158.4 15.4 %collective-permute-start = (bf16[2,8,128,128]{3,2,1,0:T(8,128)(2,1)}, bf16[2,8,128,128]{3,2,1,0:T(8,128)(2,1)S(1)}, u32[]{:S(2)}, u32[]{:S(2)}) collective-permute-start(bf16[2,8,128,128]{3,2,1,0:T(8,128)(2,1)} %fusion.136), channel_id=1, source_target_pairs={{0,8},{8,16},{16,24},{1,9},{9,17},{17,25},{2,10},{10,18},{18,26},{... | collective-permute-start | bytes 1572872 | tf_op jit(solution)/shard_map/while/body/eval_jaxpr/ppermute | solution.py:13
  174.9 14.5 %collective-permute-start = (bf16[2,8,128,128]{3,2,1,0:T(8,128)(2,1)}, bf16[2,8,128,128]{3,2,1,0:T(8,128)(2,1)S(1)}, u32[]{:S(2)}, u32[]{:S(2)}) collective-permute-start(bf16[2,8,128,128]{3,2,1,0:T(8,128)(2,1)} %fusion.136), channel_id=1, source_target_pairs={{0,8},{8,16},{16,24},{1,9},{9,17},{17,25},{2,10},{10,18},{18,26},{... | collective-permute-start | bytes 1572872 | tf_op jit(solution)/shard_map/while/body/eval_jaxpr/ppermute | solution.py:13
  267.0 20.9 %copy-start.24 = (bf16[2,512,1024]{2,1,0:T(8,128)(2,1)S(1)}, bf16[2,512,1024]{2,1,0:T(8,128)(2,1)}, u32[]{:S(2)}) copy-start(bf16[2,512,1024]{2,1,0:T(8,128)(2,1)} %param.17) | copy-start | bytes 6291460
  376.8 16.0 %copy-start.1 = (f32[128,8,2,512]{3,1,2,0:T(8,128)S(1)}, f32[128,8,2,512]{3,1,2,0:T(8,128)}, u32[]{:S(2)}) copy-start(f32[128,8,2,512]{3,1,2,0:T(8,128)} %copy.159) | copy-start | bytes 12582916
  376.8 16.0 %copy-start.3 = (f32[1024,1024]{1,0:T(8,128)S(1)}, f32[1024,1024]{1,0:T(8,128)}, u32[]{:S(2)}) copy-start(f32[1024,1024]{1,0:T(8,128)} %copy-done.2) | copy-start | bytes 12582916
  399.8 14.3 %collective-permute-start.1 = (bf16[2,8,128,128]{3,2,1,0:T(8,128)(2,1)}, bf16[2,8,128,128]{3,2,1,0:T(8,128)(2,1)S(1)}, u32[]{:S(2)}, u32[]{:S(2)}) collective-permute-start(bf16[2,8,128,128]{3,2,1,0:T(8,128)(2,1)} %fusion.137), channel_id=1, source_target_pairs={{8,0},{16,8},{24,16},{9,1},{17,9},{25,17},{10,2},{18,10},{26,18},{... | collective-permute-start | bytes 1572872 | tf_op jit(solution)/shard_map/while/body/eval_jaxpr/ppermute | solution.py:13
  415.3 13.0 %collective-permute-start.1 = (bf16[2,8,128,128]{3,2,1,0:T(8,128)(2,1)}, bf16[2,8,128,128]{3,2,1,0:T(8,128)(2,1)S(1)}, u32[]{:S(2)}, u32[]{:S(2)}) collective-permute-start(bf16[2,8,128,128]{3,2,1,0:T(8,128)(2,1)} %fusion.137), channel_id=1, source_target_pairs={{8,0},{16,8},{24,16},{9,1},{17,9},{25,17},{10,2},{18,10},{26,18},{... | collective-permute-start | bytes 1572872 | tf_op jit(solution)/shard_map/while/body/eval_jaxpr/ppermute | solution.py:13
  429.5 12.1 %collective-permute-start.1 = (bf16[2,8,128,128]{3,2,1,0:T(8,128)(2,1)}, bf16[2,8,128,128]{3,2,1,0:T(8,128)(2,1)S(1)}, u32[]{:S(2)}, u32[]{:S(2)}) collective-permute-start(bf16[2,8,128,128]{3,2,1,0:T(8,128)(2,1)} %fusion.137), channel_id=1, source_target_pairs={{8,0},{16,8},{24,16},{9,1},{17,9},{25,17},{10,2},{18,10},{26,18},{... | collective-permute-start | bytes 1572872 | tf_op jit(solution)/shard_map/while/body/eval_jaxpr/ppermute | solution.py:13
  459.8 28.1 %copy-start.9 = (f32[2,8,128,128]{3,2,1,0:T(8,128)S(1)}, f32[2,8,128,128]{3,2,1,0:T(8,128)}, u32[]{:S(2)}) copy-start(f32[2,8,128,128]{3,2,1,0:T(8,128)} %copy-done.8) | copy-start | bytes 3145732
  544.0 10.4 %copy-start.19 = (bf16[1,1024,1024]{1,2,0:T(8,128)(2,1)S(1)}, bf16[1,1024,1024]{1,2,0:T(8,128)(2,1)}, u32[]{:S(2)}) copy-start(bf16[1,1024,1024]{1,2,0:T(8,128)(2,1)} %get-tuple-element.147) | copy-start | bytes 6291460
  544.0 128.4 %reduce-scatter.13.cloned.1.call-start = ((), (), s32[]{:S(2)}) async-start(), calls=%async_computation.8 | async-start | bytes 9437184
  544.1 10.4 %copy-start.22 = (bf16[1024,1024]{1,0:T(8,128)(2,1)S(1)}, bf16[1024,1024]{1,0:T(8,128)(2,1)}, u32[]{:S(2)}) copy-start(bf16[1024,1024]{1,0:T(8,128)(2,1)} %fusion.65) | copy-start | bytes 6291460
  544.1 10.4 %copy-start.23 = (bf16[1,1024,1024]{1,2,0:T(8,128)(2,1)S(1)}, bf16[1,1024,1024]{1,2,0:T(8,128)(2,1)}, u32[]{:S(2)}) copy-start(bf16[1,1024,1024]{1,2,0:T(8,128)(2,1)} %stack_reshape.4) | copy-start | bytes 6291460
  592.7 160.4 %reduce-scatter.17.cloned.1.call-start = ((), (), s32[]{:S(2)}) async-start(), calls=%async_computation.10 | async-start | bytes 12976128
  652.4 163.2 %reduce-scatter.11.cloned.1.call-start = ((), (), s32[]{:S(2)}) async-start(), calls=%async_computation.4 | async-start | bytes 6488064 | tf_op jit(solution)/shard_map/reduce_scatter | solution.py:157
  670.0 281.8 %all-reduce.3.cloned.1.call-start = ((), (), s32[]{:S(2)}) async-start(), calls=%async_computation.11 | async-start | bytes 6946816 | tf_op jit(solution)/shard_map/psum | solution.py:164
  676.2 139.5 %copy-start.12 = (bf16[2,512,1024]{2,1,0:T(8,128)(2,1)S(1)}, bf16[2,512,1024]{2,1,0:T(8,128)(2,1)}, u32[]{:S(2)}) copy-start(bf16[2,512,1024]{2,1,0:T(8,128)(2,1)} %param.11) | copy-start | bytes 6291460
  815.7 15.1 %copy-start.4 = (f32[1024,1024]{1,0:T(8,128)S(1)}, f32[1024,1024]{1,0:T(8,128)}, u32[]{:S(2)}) copy-start(f32[1024,1024]{1,0:T(8,128)} %copy-done.2) | copy-start | bytes 12582916
  (27 other events, 159.0 us)
Sparse Core Ops, SparseCore 0:
  10.4 67.9 all-gather.6
  80.9 67.6 all-gather.8
  150.5 43.3 all-gather.10
  544.1 40.0 reduce-scatter.14
  592.9 70.0 reduce-scatter.12
  666.3 86.8 reduce-scatter.16
  756.6 59.0 reduce-scatter.10
  819.1 132.6 all-reduce.2
where the time goes:
time: 978 us; the launch traced here: 967 us
  waiting for transfers between devices  357 us (37%)
  matrix products  343 us (35%)
  local copies, waits for them, and re-layouts  187 us (19%)
  other arithmetic  47.8 us (5%)
  starting transfers between devices  16.2 us (2%)
  between operations  15.2 us (2%)
    psum x1, waiting for transfers between devices, reduce_grads(): lax.psum(pieces[2].astype(jnp.bfloat16), 'seq').astype(jnp.float32)  104 us
    unnamed x89, local copies, waits for them, and re-layouts  98 us
    unnamed x11, waiting for transfers between devices  77.1 us
    ppermute x6, waiting for transfers between devices, passed_along(): lax.ppermute(value, axis, [(source, source + steps) for source in range(l...  68.6 us
    reduce_scatter x1, waiting for transfers between devices, reduce_grads(): lax.psum_scatter(terms[3].astype(jnp.bfloat16), 'dp', scatter_dimension=0...  56 us
    all_gather x1, waiting for transfers between devices, local(): mixer_full = lax.all_gather(gathered[0], 'dp', axis=1, tiled=True)  51.9 us
    dot_general x1, matrix products, block_back(): jnp.einsum('rhts,rshd->rthd', score_grad, per_head_keys, precision=FULL_P...  28.1 us
    dot_general x1, matrix products, block_out(): jnp.einsum('rhts,rshe->rthe', scores, per_head_values, precision=FULL_PRE...  23.7 us
  transfers between devices with their start and end apart: 14, of which 10 were waited for; matrix products, arithmetic and copies ran while one was open for 36% of the time, Pallas kernels for 0%

commit v1 on v0

--- a/solution.py
+++ b/solution.py
@@ -5,6 +5,18 @@
 
 EPS = 1e-06
 FULL_PRECISION = lax.Precision.HIGHEST
+
+
+def collect(value, axis, dim):
+    ways, here = (lax.axis_size(axis), lax.axis_index(axis))
+    grown, reach = (value, 1)
+    while reach < ways:
+        theirs = lax.ppermute(grown, axis, [(d, d ^ reach) for d in range(ways)])
+        mine_first = jnp.concatenate([grown, theirs], axis=dim)
+        theirs_first = jnp.concatenate([theirs, grown], axis=dim)
+        grown = jnp.where(here & reach == 0, mine_first, theirs_first)
+        reach = 2 * reach
+    return grown
 
 
 def passed_along(value, axis, steps):
@@ -190,7 +202,7 @@
         channel_in_weights[layer_index].astype(jnp.bfloat16),
         channel_out_weights[layer_index].astype(jnp.bfloat16),
     )
-    mixer_full = lax.all_gather(gathered[0], "dp", axis=1, tiled=True)
+    mixer_full = collect(gathered[0], "dp", 1)
     channel_full = lax.all_gather(gathered[1], "dp", axis=1, tiled=True)
     down_full = lax.all_gather(gathered[2], "dp", axis=0, tiled=True)
     normed, factor_in = rms_norm(resid)

time: 978 us -> 1170 us (1.20)
  waiting for transfers between devices: 357 us -> 529 us
  other arithmetic: 47.8 us -> 62.1 us
    ppermute x0 -> x3, waiting for transfers between devices: none -> 233 us  [collect(): theirs = lax.ppermute(grown, axis, [(d, d ^ reach) for d in range(ways)])]
    all_gather x1 -> x0, waiting for transfers between devices: 51.9 us -> none  [local(): mixer_full = lax.all_gather(gathered[0], 'dp', axis=1, tiled=True)]
    select_n x0 -> x3, other arithmetic: none -> 21.4 us  [collect(): grown = jnp.where(here & reach == 0, mine_first, theirs_first)]
    ppermute x6, waiting for transfers between devices: 68.6 us -> 55.4 us  [passed_along(): lax.ppermute(value, axis, [(source, source + steps) for source in range(l...]
    unnamed x11 -> x10, waiting for transfers between devices: 77.1 us -> 81.6 us
    unnamed x89 -> x97, local copies, waits for them, and re-layouts: 98 us -> 102 us
  transfers between devices with their start and end apart: 14 -> 16, of which waited for: 10 -> 12; matrix products, arithmetic and copies ran while one was open for 36% -> 31% of each run, Pallas kernels for 0% -> 0%
where the time goes in v1:
time: 1170 us; the launch traced here: 1160 us
  waiting for transfers between devices  529 us (45%)
  matrix products  338 us (29%)
  local copies, waits for them, and re-layouts  191 us (16%)
  other arithmetic  62.1 us (5%)
  starting transfers between devices  21.7 us (2%)
  between operations  15.2 us (1%)
    ppermute x3, waiting for transfers between devices, collect(): theirs = lax.ppermute(grown, axis, [(d, d ^ reach) for d in range(ways)])  233 us
    psum x1, waiting for transfers between devices, reduce_grads(): lax.psum(pieces[2].astype(jnp.bfloat16), 'seq').astype(jnp.float32)  104 us
    unnamed x97, local copies, waits for them, and re-layouts  102 us
    unnamed x10, waiting for transfers between devices  81.6 us
    reduce_scatter x1, waiting for transfers between devices, reduce_grads(): lax.psum_scatter(terms[3].astype(jnp.bfloat16), 'dp', scatter_dimension=0...  55.9 us
    ppermute x6, waiting for transfers between devices, passed_along(): lax.ppermute(value, axis, [(source, source + steps) for source in range(l...  55.4 us
    dot_general x1, matrix products, block_back(): jnp.einsum('rhts,rshd->rthd', score_grad, per_head_keys, precision=FULL_P...  28 us
    dot_general x1, matrix products, block_out(): jnp.einsum('rhts,rshe->rthe', scores, per_head_values, precision=FULL_PRE...  23.7 us
  transfers between devices with their start and end apart: 16, of which 12 were waited for; matrix products, arithmetic and copies ran while one was open for 31% of the time, Pallas kernels for 0%

profile of v1, /device:TPU:0, one launch (start us, length us, event | category | flops | bytes accessed | tf_op | source)
XLA Modules:
  0.0 1157.6 jit_solution(8983483292650208063)
XLA Ops:
  20.4 103.7 %collective-permute-done.3 = bf16[5,256,1024]{1,2,0:T(8,128)(2,1)} collective-permute-done((bf16[5,256,1024]{1,2,0:T(8,128)(2,1)}, bf16[5,256,1024]{1,2,0:T(8,128)(2,1)}, u32[]{:S(2)}, u32[]{:S(2)}) %collective-permute-start.3) | collective-permute-done | bytes 2621472 | tf_op jit(solution)/shard_map/ppermute | solution.py:14
  142.7 126.2 %collective-permute-done.4 = bf16[5,512,1024]{1,2,0:T(8,128)(2,1)} collective-permute-done((bf16[5,512,1024]{1,2,0:T(8,128)(2,1)}, bf16[5,512,1024]{1,2,0:T(8,128)(2,1)}, u32[]{:S(2)}, u32[]{:S(2)}) %collective-permute-start.4) | collective-permute-done | bytes 5242912 | tf_op jit(solution)/shard_map/ppermute | solution.py:14
  268.9 11.9 %maximum_select_fusion = bf16[5,1024,1024]{1,2,0:T(8,128)(2,1)S(1)} fusion(bf16[5,512,1024]{1,2,0:T(8,128)(2,1)} %collective-permute-done.4, bf16[5,512,1024]{1,2,0:T(8,128)(2,1)} %maximum_select_fusion.1, pred[]{:T(512)S(6)} %eq.54), kind=kLoop, calls=%fused_computation.29 | loop fusion | flops 47185920 | bytes 20971520 | tf_op jit(solution)/shard_map/jit(_where)/select_n | solution.py:17
  342.2 36.5 %while.22 = (s32[]{:T(128)}, f32[2,8,128,128]{3,2,1,0:T(8,128)S(1)}, f32[2,8,128,128]{3,2,1,0:T(8,128)S(1)}, f32[8]{0:T(128)S(1)}, pred[2]{0:T(512)(128)(4,1)S(1)}, /*index=5*/s32[]{:T(128)}, s32[]{:T(128)}) while((s32[]{:T(128)}, f32[2,8,128,128]{3,2,1,0:T(8,128)S(1)}, f32[2,8,128,128]{3,2,1,0:T(8,128)S(1)}, f32[8]{0:T(128)S(1)}, ...), condition=%wide.region_5.6_spmd.clone, body=%wide.region_4.5_spmd.clone.sunk | while | flops 1310739 | bytes 6291745 | solution.py:146
  388.0 17.3 %fusion.119 = f32[2,8,512,512]{3,2,1,0:T(8,128)} fusion(f32[2,512,8,128]{1,0,3,2:T(2,128)S(1)} %copy-done.14, f32[2,512,8,128]{1,0,3,2:T(2,128)S(1)} %copy-done.13), kind=kOutput, calls=%fused_computation.168 | convolution fusion | flops 6450839552 | bytes 25165824 | tf_op jit(solution)/shard_map/rthd,rshd->rhts/dot_general | solution.py:88
  405.3 23.7 %multiply_reduce_fusion.2 = (f32[2,512]{1,0:T(2,128)S(1)}, f32[2,512,8,128]{1,3,2,0:T(8,128)}) fusion(f32[2,512,8]{1,2,0:T(8,128)S(1)} %get-tuple-element.166, f32[2,8,128,512]{3,2,1,0:T(8,128)} %fusion.120, f32[2,512,8,128]{3,1,2,0:T(8,128)} %copy.119, f32[2,8,512,512]{3,2,1,0:T(8,128)} %fusion.119, f32[8,512,512]{2,1,0:T(8,128)} %multiply_exponential_fusion, ...), kind=kOutput, calls=%fused_computation.101 | convolution fusion | flops 6455032832 | bytes 38309888 | tf_op jit(solution)/shard_map/rhts,rshe->rthe/dot_general | solution.py:91
  456.3 20.9 %fusion.19 = f32[2,1024,2816]{2,1,0:T(8,128)} fusion(bf16[1,2,1024,2816]{3,2,1,0:T(8,128)(2,1)} %all-gather.5.cloned.1.call-done, f32[1024,1024]{1,0:T(8,128)} %get-tuple-element.159, f32[1024]{0:T(1024)S(1)} %get-tuple-element.149), kind=kOutput, calls=%fused_computation.30 | convolution fusion | flops 11813257216 | bytes 38801408 | tf_op jit(solution)/shard_map/nd,kdf->knf/dot_general | solution.py:231
  477.2 14.9 %fusion.42 = (bf16[1,1024,2816]{2,1,0:T(8,128)(2,1)}, bf16[1,1024,2816]{2,1,0:T(8,128)(2,1)}) fusion(f32[2,1024,2816]{2,1,0:T(8,128)} %fusion.19, bf16[1024,1024]{1,0:T(8,128)(2,1)S(1)} %bitcast.231, bf16[1,2816,1024]{2,1,0:T(8,128)(2,1)} %all-gather.7.cloned.1.call-done), kind=kOutput, calls=%fused_computation.53 | convolution fusion | flops 5922881536 | bytes 42467328 | tf_op jit(solution)/shard_map/nd,fd->nf/dot_general | solution.py:297
  492.1 20.3 %fusion.63 = (f32[1024]{0:T(1024)S(1)}, f32[1024,1024,1]{1,0,2:T(8,128)}) fusion(f32[1024,1024]{1,0:T(8,128)} %get-tuple-element.159, bf16[1,2,1024,2816]{3,2,1,0:T(8,128)(2,1)} %all-gather.5.cloned.1.call-done, bf16[1,1024,2816]{2,1,0:T(8,128)(2,1)} %get-tuple-element.140, bf16[1,1024,2816]{2,1,0:T(8,128)(2,1)} %get-tuple-element.139), kind=kOutput, calls=%fused_computation.81 | convolution fusion | flops 11819023360 | bytes 31461376 | tf_op jit(solution)/shard_map/knf,kdf->nd/dot_general | solution.py:305
  537.3 19.9 %fusion.8 = f32[2,8,128,512]{3,2,1,0:T(8,128)} fusion(f32[2,8,512,512]{3,2,1,0:T(8,128)} %fusion.119, f32[8,512,512]{2,1,0:T(8,128)} %multiply_exponential_fusion, pred[2,512,512]{2,1,0:T(8,128)(4,1)S(1)} %copy-done.17, f32[2,512,8,128]{1,0,3,2:T(2,128)} %reshape.344), kind=kOutput, calls=%fused_computation.12 | convolution fusion | flops 6450839552 | bytes 34078720 | tf_op jit(solution)/shard_map/rhts,rthe->rshe/dot_general | solution.py:131
  566.1 16.0 %fusion.75 = f32[2,8,512,512]{3,2,1,0:T(8,128)} fusion(f32[2,512,8,128]{3,1,2,0:T(8,128)S(1)} %copy-done.5, f32[2,512,8,128]{1,0,3,2:T(2,128)S(1)} %copy-done.6), kind=kOutput, calls=%fused_computation.109 | convolution fusion | flops 6442450944 | bytes 25165824 | tf_op jit(solution)/shard_map/rthe,rshe->rhts/dot_general | solution.py:117
  588.0 39.9 %while.23 = (s32[]{:T(128)}, f32[2,8,128,128]{3,2,1,0:T(8,128)S(1)}, f32[2,8,128,128]{3,2,1,0:T(8,128)S(1)}, f32[8]{0:T(128)S(1)}, pred[2]{0:T(512)(128)(4,1)S(1)}, /*index=5*/s32[]{:T(128)}, s32[]{:T(128)}) while((s32[]{:T(128)}, f32[2,8,128,128]{3,2,1,0:T(8,128)S(1)}, f32[2,8,128,128]{3,2,1,0:T(8,128)S(1)}, f32[8]{0:T(128)S(1)}, ...), condition=%wide.region_11.12_spmd.clone, body=%wide.region_10.11_spmd.clone.sunk | while | flops 1310739 | bytes 6291745 | solution.py:155
  645.9 28.0 %fusion.11 = f32[2,8,128,512]{3,2,1,0:T(8,128)} fusion(f32[2,8,512,512]{3,2,1,0:T(8,128)} %fusion.75, f32[8,512,512]{2,1,0:T(8,128)} %multiply_exponential_fusion, pred[2,512,512]{2,1,0:T(8,128)(4,1)S(1)} %copy-done.17, f32[2,512,8,128]{1,0,3,2:T(2,128)} %squeeze.13), kind=kOutput, calls=%fused_computation.15 | convolution fusion | flops 6455033856 | bytes 34078720 | tf_op jit(solution)/shard_map/rhts,rshd->rthd/dot_general | solution.py:119
  694.3 21.6 %fusion.58 = f32[2,512,8,128]{1,3,2,0:T(8,128)} fusion(f32[2,8,128,512]{3,2,1,0:T(8,128)} %fusion.124, f32[2,8,512,512]{3,2,1,0:T(8,128)} %fusion.75, f32[8,512,512]{2,1,0:T(8,128)} %multiply_exponential_fusion, pred[2,512,512]{2,1,0:T(8,128)(4,1)S(1)} %copy-done.17, f32[2,512,8]{1,2,0:T(8,128)S(1)} %copy-done.32, f32[2,512,8,128]{1,0,3,2:T(2,128)} %squeeze.12), kind=kOutput, calls=%fused_computation.72 | convolution fusion | flops 6457131008 | bytes 38305792 | tf_op jit(solution)/shard_map/rhts,rthd->rshd/dot_general | solution.py:125
  751.1 15.1 %copy.151 = bf16[4,1024,1024]{2,0,1:T(4,128)(2,1)} copy(bf16[4,1024,1024]{1,2,0:T(8,128)(2,1)} %convert_bitcast_fusion.1) | data formatting | bytes 16777216
  766.2 12.2 %copy.160 = bf16[128,8,4,1024]{3,1,2,0:T(8,128)(2,1)} copy(bf16[128,8,4,1024]{3,2,1,0:T(4,128)(2,1)} %bitcast.224) | data formatting | bytes 16777216
  778.5 19.5 %convert_bitcast_fusion = bf16[2,1024,2816]{1,2,0:T(8,128)(2,1)} fusion(bf16[1,1024,2816]{2,1,0:T(8,128)(2,1)} %get-tuple-element.140, bf16[1,1024,2816]{2,1,0:T(8,128)(2,1)} %get-tuple-element.139, f32[1024,1024]{1,0:T(8,128)} %get-tuple-element.159, f32[1024]{0:T(1024)S(1)} %get-tuple-element.149), kind=kOutput, calls=%fused_computation.28 | convolution fusion | flops 11824791552 | bytes 27267072 | tf_op jit(solution)/shard_map/nd,knf->kdf/dot_general | solution.py:302
  798.0 29.2 %copy.155 = bf16[2,1024,2816]{2,0,1:T(2,128)(2,1)} copy(bf16[2,1024,2816]{1,2,0:T(8,128)(2,1)} %convert_bitcast_fusion) | data formatting | bytes 23068672
  840.5 15.8 %fusion.46 = bf16[2816,1024]{1,0:T(8,128)(2,1)} fusion(bf16[1024,1024]{1,0:T(8,128)(2,1)S(1)} %bitcast.232, f32[2,1024,2816]{2,1,0:T(8,128)} %fusion.19), kind=kOutput, calls=%fused_computation.57 | convolution fusion | flops 5914230784 | bytes 30932992 | tf_op jit(solution)/shard_map/nf,nd->fd/dot_general | solution.py:295
  862.5 81.5 %reduce-scatter.17.cloned.1.call-done = bf16[128,5632]{1,0:T(8,128)(2,1)} async-done(((bf16[1024,5632]{1,0:T(8,128)(2,1)}), bf16[128,5632]{1,0:T(8,128)(2,1)}) %reduce-scatter.17.cloned.1.call-update) | async-done | bytes 1441808
  950.5 55.9 %reduce-scatter.11.cloned.1.call-done = bf16[352,1024]{1,0:T(8,128)(2,1)} async-done(((bf16[2816,1024]{1,0:T(8,128)(2,1)}), bf16[352,1024]{1,0:T(8,128)(2,1)}) %reduce-scatter.11.cloned.1.call-update) | async-done | bytes 720912 | tf_op jit(solution)/shard_map/reduce_scatter | solution.py:169
  1006.4 15.1 %fusion.55 = (f32[1024]{0:T(1024)S(1)}, f32[1024,1024,1]{1,0,2:T(8,128)S(1)}) fusion(bf16[2,512,1024]{2,1,0:T(8,128)(2,1)S(1)} %copy-done.12, bf16[5,1024,1024]{1,2,0:T(8,128)(2,1)} %copy-done.16, bf16[1,1024,1024]{1,2,0:T(8,128)(2,1)} %get-tuple-element.147, bf16[1,1024,1024]{1,2,0:T(8,128)(2,1)} %stack_reshape.4, bf16[1,1024,1024]{1,2,0:T(8,128)(2,1)} %copy-done.23, ...), kind=kOutput, calls=%fused_computation.67 | convolution fusion | flops 8605662208 | bytes 23072768 | tf_op jit(solution)/shard_map/kne,kde->nd/dot_general | solution.py:345
  1025.1 13.7 %add_convert_fusion = bf16[1024,1024]{1,0:T(8,128)(2,1)} fusion(f32[1024,1024]{1,0:T(8,128)S(1)} %copy-done.19, bf16[1,2816,1024]{2,1,0:T(8,128)(2,1)} %all-gather.7.cloned.1.call-done, f32[2,1024,2816]{2,1,0:T(8,128)} %fusion.19), kind=kOutput, calls=%fused_computation.97 | convolution fusion | flops 5913444352 | bytes 35127296 | tf_op jit(solution)/shard_map/dot_general | solution.py:29
  1038.8 103.7 %all-reduce.3.cloned.1.call-done = (bf16[1,2,128,2816]{2,3,1,0:T(8,128)(2,1)}, bf16[1,128,1024]{1,2,0:T(8,128)(2,1)}, bf16[4,128,1024]{1,2,0:T(8,128)(2,1)}, bf16[1,352,1024]{2,1,0:T(8,128)(2,1)}) async-done(((bf16[1,2,128,2816]{2,3,1,0:T(8,128)(2,1)}, bf16[1,128,1024]{1,2,0:T(8,128)(2,1)}, bf16[4,128,1024]{1,2,0:T(8,128)(2,1)}, bf16[1,352,1024]{2,1,0:T(8,128)(2,1)}), (bf16[1,2,128,2816]{2,3,1,0:T(8,128)(2,1)}, ...) | async-done | bytes 3473424 | tf_op jit(solution)/shard_map/psum | solution.py:176
  (207 shorter events, 355.8 us)
Async XLA Ops:
  7.2 449.1 %all-gather.5.cloned.1.call-start = ((), (), s32[]{:S(2)}) async-start(), calls=%async_computation.5 | async-start | bytes 12976128 | tf_op jit(solution)/shard_map/all_gather | solution.py:206
  10.3 466.9 %all-gather.7.cloned.1.call-start = ((), (), s32[]{:S(2)}) async-start(), calls=%async_computation.6 | async-start | bytes 6488064 | tf_op jit(solution)/shard_map/all_gather | solution.py:207
  12.4 3.2 collective-permute-start.2
  17.5 106.6 %collective-permute-start.3 = (bf16[5,256,1024]{1,2,0:T(8,128)(2,1)}, bf16[5,256,1024]{1,2,0:T(8,128)(2,1)}, u32[]{:S(2)}, u32[]{:S(2)}) collective-permute-start(bf16[5,256,1024]{1,2,0:T(8,128)(2,1)} %maximum_select_fusion.2), channel_id=1, source_target_pairs={{0,2},{1,3},{2,0},{3,1},{4,6},{5,7},{6,4},{7,5},{8,10},{9,11},{10,... | collective-permute-start | bytes 7864328 | tf_op jit(solution)/shard_map/ppermute | solution.py:14
  20.4 113.3 %copy-start.29 = (f32[1,352,1024]{2,1,0:T(8,128)S(1)}, f32[1,352,1024]{2,1,0:T(8,128)}, u32[]{:S(2)}) copy-start(f32[1,352,1024]{2,1,0:T(8,128)} %param.14) | copy-start | bytes 4325380
  20.4 114.3 %copy-start.10 = (bf16[2,512,1024]{2,1,0:T(8,128)(2,1)S(1)}, bf16[2,512,1024]{2,1,0:T(8,128)(2,1)}, u32[]{:S(2)}) copy-start(bf16[2,512,1024]{2,1,0:T(8,128)(2,1)} %param.11) | copy-start | bytes 6291460
  131.7 137.2 %collective-permute-start.4 = (bf16[5,512,1024]{1,2,0:T(8,128)(2,1)}, bf16[5,512,1024]{1,2,0:T(8,128)(2,1)}, u32[]{:S(2)}, u32[]{:S(2)}) collective-permute-start(bf16[5,512,1024]{1,2,0:T(8,128)(2,1)} %maximum_select_fusion.1), channel_id=1, source_target_pairs={{0,4},{1,5},{2,6},{3,7},{4,0},{5,1},{6,2},{7,3},{8,12},{9,13},{10,... | collective-permute-start | bytes 15728648 | tf_op jit(solution)/shard_map/ppermute | solution.py:14
  134.6 722.3 %reduce-scatter.15.cloned.1.call-start = ((), (), s32[]{:S(2)}) async-start(), calls=%async_computation.8 | async-start | bytes 2359296
  136.6 197.1 %copy-start.31 = (f32[2,512,8]{1,2,0:T(8,128)}, f32[2,512,8]{1,2,0:T(8,128)S(1)}, u32[]{:S(2)}) copy-start(f32[2,512,8]{1,2,0:T(8,128)S(1)} %get-tuple-element.167) | copy-start | bytes 98308
  138.2 142.5 %copy-start.24 = (bf16[1024,1024]{1,0:T(8,128)(2,1)}, bf16[1024,1024]{1,0:T(8,128)(2,1)S(1)}, u32[]{:S(2)}) copy-start(bf16[1024,1024]{1,0:T(8,128)(2,1)S(1)} %fusion.66) | copy-start | bytes 6291460
  342.5 12.0 %collective-permute-start = (bf16[2,8,128,128]{3,2,1,0:T(8,128)(2,1)S(1)}, bf16[2,8,128,128]{3,2,1,0:T(8,128)(2,1)S(1)}, u32[]{:S(2)}, u32[]{:S(2)}) collective-permute-start(bf16[2,8,128,128]{3,2,1,0:T(8,128)(2,1)S(1)} %fusion.138), channel_id=1, source_target_pairs={{0,8},{8,16},{16,24},{1,9},{9,17},{17,25},{2,10},{10,18},{18,26},{... | collective-permute-start | bytes 1572872 | tf_op jit(solution)/shard_map/while/body/eval_jaxpr/ppermute | solution.py:25
  355.0 12.1 %collective-permute-start = (bf16[2,8,128,128]{3,2,1,0:T(8,128)(2,1)S(1)}, bf16[2,8,128,128]{3,2,1,0:T(8,128)(2,1)S(1)}, u32[]{:S(2)}, u32[]{:S(2)}) collective-permute-start(bf16[2,8,128,128]{3,2,1,0:T(8,128)(2,1)S(1)} %fusion.138), channel_id=1, source_target_pairs={{0,8},{8,16},{16,24},{1,9},{9,17},{17,25},{2,10},{10,18},{18,26},{... | collective-permute-start | bytes 1572872 | tf_op jit(solution)/shard_map/while/body/eval_jaxpr/ppermute | solution.py:25
  367.5 11.2 collective-permute-start
  388.0 17.3 %copy-start.17 = (pred[2,512,512]{2,1,0:T(8,128)(4,1)S(1)}, pred[2,512,512]{2,1,0:T(8,128)(4,1)}, u32[]{:S(2)}) copy-start(pred[2,512,512]{2,1,0:T(8,128)(4,1)} %compare_and_fusion) | copy-start | bytes 1572868
  456.3 20.9 %copy-start.27 = (bf16[2,512,1024]{2,1,0:T(8,128)(2,1)S(1)}, bf16[2,512,1024]{2,1,0:T(8,128)(2,1)}, u32[]{:S(2)}) copy-start(bf16[2,512,1024]{2,1,0:T(8,128)(2,1)} %param.17) | copy-start | bytes 6291460
  589.1 11.8 %collective-permute-start.1 = (bf16[2,8,128,128]{3,2,1,0:T(8,128)(2,1)}, bf16[2,8,128,128]{3,2,1,0:T(8,128)(2,1)S(1)}, u32[]{:S(2)}, u32[]{:S(2)}) collective-permute-start(bf16[2,8,128,128]{3,2,1,0:T(8,128)(2,1)} %fusion.139), channel_id=1, source_target_pairs={{8,0},{16,8},{24,16},{9,1},{17,9},{25,17},{10,2},{18,10},{26,18},{... | collective-permute-start | bytes 1572872 | tf_op jit(solution)/shard_map/while/body/eval_jaxpr/ppermute | solution.py:25
  602.1 12.7 %collective-permute-start.1 = (bf16[2,8,128,128]{3,2,1,0:T(8,128)(2,1)}, bf16[2,8,128,128]{3,2,1,0:T(8,128)(2,1)S(1)}, u32[]{:S(2)}, u32[]{:S(2)}) collective-permute-start(bf16[2,8,128,128]{3,2,1,0:T(8,128)(2,1)} %fusion.139), channel_id=1, source_target_pairs={{8,0},{16,8},{24,16},{9,1},{17,9},{25,17},{10,2},{18,10},{26,18},{... | collective-permute-start | bytes 1572872 | tf_op jit(solution)/shard_map/while/body/eval_jaxpr/ppermute | solution.py:25
  616.0 11.6 %collective-permute-start.1 = (bf16[2,8,128,128]{3,2,1,0:T(8,128)(2,1)}, bf16[2,8,128,128]{3,2,1,0:T(8,128)(2,1)S(1)}, u32[]{:S(2)}, u32[]{:S(2)}) collective-permute-start(bf16[2,8,128,128]{3,2,1,0:T(8,128)(2,1)} %fusion.139), channel_id=1, source_target_pairs={{8,0},{16,8},{24,16},{9,1},{17,9},{25,17},{10,2},{18,10},{26,18},{... | collective-permute-start | bytes 1572872 | tf_op jit(solution)/shard_map/while/body/eval_jaxpr/ppermute | solution.py:25
  645.9 28.1 %copy-start.9 = (f32[2,8,128,128]{3,2,1,0:T(8,128)S(1)}, f32[2,8,128,128]{3,2,1,0:T(8,128)}, u32[]{:S(2)}) copy-start(f32[2,8,128,128]{3,2,1,0:T(8,128)} %copy-done.8) | copy-start | bytes 3145732
  730.0 128.7 %reduce-scatter.13.cloned.1.call-start = ((), (), s32[]{:S(2)}) async-start(), calls=%async_computation.7 | async-start | bytes 9437184
  778.4 165.6 %reduce-scatter.17.cloned.1.call-start = ((), (), s32[]{:S(2)}) async-start(), calls=%async_computation.9 | async-start | bytes 12976128
  838.6 167.7 %reduce-scatter.11.cloned.1.call-start = ((), (), s32[]{:S(2)}) async-start(), calls=%async_computation.4 | async-start | bytes 6488064 | tf_op jit(solution)/shard_map/reduce_scatter | solution.py:169
  856.3 286.1 %all-reduce.3.cloned.1.call-start = ((), (), s32[]{:S(2)}) async-start(), calls=%async_computation.10 | async-start | bytes 6946816 | tf_op jit(solution)/shard_map/psum | solution.py:176
  862.5 143.9 %copy-start.12 = (bf16[2,512,1024]{2,1,0:T(8,128)(2,1)S(1)}, bf16[2,512,1024]{2,1,0:T(8,128)(2,1)}, u32[]{:S(2)}) copy-start(bf16[2,512,1024]{2,1,0:T(8,128)(2,1)} %param.11) | copy-start | bytes 6291460
  (33 other events, 240.0 us)
Sparse Core Ops, SparseCore 0:
  10.5 115.3 all-gather.4
  134.8 67.0 all-gather.6
  730.1 45.0 reduce-scatter.14
  778.9 74.8 reduce-scatter.12
  857.2 86.7 reduce-scatter.16
  947.3 59.0 reduce-scatter.10
  1009.8 132.6 all-reduce.2
